TPU v7x, 32 devices: a whole 2x2x4 slice. The times are simulated.
32 devices in a mesh: grp: 2 (over x), seq: 8 (over z, y), ch: 2 (over core).
Axes of the slice: x: 2, y: 2, z: 4, core: 2. Of those that a mesh axis runs over, the one named last changes fastest.
Arguments:
- seq_in: bfloat16 [4096, 1536], P(('grp', 'seq'), 'ch'), parts along dimension 0, may hold values from -6 to 6
- conv_gain: float32 [2, 1536], P(None, 'ch'), may hold values from 0.5 to 1.5
- dw_kernel: float32 [2, 5, 1536], P(None, None, 'ch'), may hold values from -2.5 to 2.5
- mix_weight: bfloat16 [2, 1536, 1536], P(None, 'ch'), may hold values from -0.15625 to 0.15625
- attn_gain: float32 [1536], P('ch'), may hold values from 0.8 to 100, as said below
- q_weight: bfloat16 [1536, 1024], P(None, 'ch'), may hold values from -0.15625 to 0.15625
- kv_weight: bfloat16 [1536, 2, 256], P(None, None, 'ch'), may hold values from -0.15625 to 0.15625
- out_weight: bfloat16 [1024, 1536], P('ch'), may hold values from -0.1875 to 0.1875
Outputs:
- seq_out: bfloat16 [4096, 1536], P(('grp', 'seq'), 'ch'), parts along dimension 0
There are 2 independent parts, one for each index of `grp`. A program takes and returns all parts, laid end to end along the dimension named above; an argument that names none is the same for every part. Nothing has to cross between parts.
Inputs may be any that keep to these rules, and one draw needn't show every extreme that they name: `attn_gain`: gains of the attention norm are positive.
All inputs are finite; a program needn't handle non-finite values.
Results may differ from a plain program's by a relative error of at most 0.03.
The roundings to bfloat16 on the way count: a program that leaves them out, or rounds other values in their place, can miss the bound.
Values may be sent and summed in bfloat16 or wider, within the bound.
No kernel may reach another device: no remote copies, remote signals or barrier semaphores. Data moves between devices by JAX's collectives and lax.ppermute only.
A program may use at most 64 MiB of HBM per device.

v0:
```python
import math
import jax
import jax.numpy as jnp
from jax import lax
from jax.sharding import PartitionSpec as P

HD = 128
EPSILON = 1e-06


def extended(shard, sides, width):
    for axis, dim in sides:
        size, length = (lax.axis_size(axis), shard.shape[dim])
        up = [(i, (i + 1) % size) for i in range(size - 1)]
        down = [(j, i) for i, j in up]
        last = lax.slice_in_dim(shard, length - width, length, axis=dim)
        initial = lax.slice_in_dim(shard, 0, width, axis=dim)
        before = lax.ppermute(last, axis, up)
        after = lax.ppermute(initial, axis, down)
        shard = jnp.concatenate([before, shard, after], axis=dim)
    return shard


def row_normalize(hidden, gain):
    channels = hidden.shape[1] * lax.axis_size("ch")
    squares = lax.psum(jnp.sum(hidden * hidden, axis=1), "ch")
    return hidden * lax.rsqrt(squares[:, None] / channels + EPSILON) * gain


def dilated_sum(padded, kernels, dilation, row_count):
    summed = padded[0:row_count] * kernels[0]
    for tap_index in range(1, kernels.shape[0]):
        summed = (
            summed
            + padded[tap_index * dilation : tap_index * dilation + row_count] * kernels[tap_index]
        )
    return summed


def channel_mix(gelu_output, weight):
    return lax.psum_scatter(
        jnp.dot(gelu_output, weight, preferred_element_type=jnp.float32),
        "ch",
        scatter_dimension=1,
        tiled=True,
    )


def local(seq_in, conv_gain, dw_kernel, mix_weight, attn_gain, q_weight, kv_weight, out_weight):
    local_rows = seq_in.shape[0]
    kernel_half = dw_kernel.shape[1] // 2
    dilation_list = [local_rows // 8, local_rows // 4]
    first_reach = kernel_half * dilation_list[0]
    second_reach = kernel_half * dilation_list[1]
    widened = extended(seq_in, (("seq", 0),), first_reach + second_reach).astype(jnp.float32)
    normalized_rows = row_normalize(widened, conv_gain[0])
    leading_rows = local_rows + 2 * second_reach
    summed = dilated_sum(normalized_rows, dw_kernel[0], dilation_list[0], leading_rows)
    gelu_output = jax.nn.gelu(summed, approximate=True).astype(jnp.bfloat16)
    middle = widened[first_reach : first_reach + leading_rows] + channel_mix(
        gelu_output, mix_weight[0]
    )
    position = (
        lax.axis_index("seq") * local_rows
        - second_reach
        + lax.broadcasted_iota(jnp.int32, (leading_rows,), 0)
    )
    inside = (position >= 0) & (position < local_rows * lax.axis_size("seq"))
    middle = jnp.where(inside[:, None], middle, 0.0)
    normalized_rows = row_normalize(middle, conv_gain[1])
    summed = dilated_sum(normalized_rows, dw_kernel[1], dilation_list[1], local_rows)
    gelu_output = jax.nn.gelu(summed, approximate=True).astype(jnp.bfloat16)
    hidden = middle[second_reach : second_reach + local_rows] + channel_mix(
        gelu_output, mix_weight[1]
    )
    normalized_rows = row_normalize(hidden, attn_gain).astype(jnp.bfloat16)
    features = lax.all_gather(normalized_rows, "ch", axis=1, tiled=True)
    query_rows = jnp.dot(features, q_weight, preferred_element_type=jnp.float32).astype(
        jnp.bfloat16
    )
    kv_width = kv_weight.shape[2]
    pairs = jnp.dot(
        features,
        kv_weight.reshape(kv_weight.shape[0], 2 * kv_width),
        preferred_element_type=jnp.float32,
    ).astype(jnp.bfloat16)
    keys_local = pairs[:, :kv_width]
    values_local = pairs[:, kv_width:]
    kv_local = kv_width // HD
    group_size = q_weight.shape[1] // HD // kv_local
    query_grid = query_rows.reshape(local_rows, kv_local, group_size, HD)
    scale = 1.0 / math.sqrt(HD)

    def key_block(carry, block):
        running_max, running_sum, context = carry
        key_part, value_part = block
        scores = (
            jnp.einsum("pkgd,skd->kgps", query_grid, key_part, preferred_element_type=jnp.float32)
            * scale
        )
        new_max = jnp.maximum(running_max, jnp.max(scores, axis=-1))
        factor = jnp.exp(running_max - new_max)
        probs = jnp.exp(scores - new_max[..., None])
        running_sum = running_sum * factor + jnp.sum(probs, axis=-1)
        update = jnp.einsum(
            "kgps,skd->kgpd",
            probs.astype(jnp.bfloat16),
            value_part,
            preferred_element_type=jnp.float32,
        )
        context = context * factor[..., None] + update
        return ((new_max, running_sum, context), None)

    initial = (
        jnp.full((kv_local, group_size, local_rows), -1e30, jnp.float32),
        jnp.zeros((kv_local, group_size, local_rows), jnp.float32),
        jnp.zeros((kv_local, group_size, local_rows, HD), jnp.float32),
    )
    carry = initial
    key_piece = lax.all_gather(keys_local, "seq", axis=0, tiled=True)
    value_piece = lax.all_gather(values_local, "seq", axis=0, tiled=True)
    key_count = key_piece.shape[0]
    block_len = math.gcd(key_count, 512)
    blocks = (
        key_piece.reshape(key_count // block_len, block_len, kv_local, HD),
        value_piece.reshape(key_count // block_len, block_len, kv_local, HD),
    )
    carry, unused = lax.scan(key_block, carry, blocks)
    running_max, running_sum, context = carry
    attended = (context / running_sum[..., None]).astype(jnp.bfloat16)
    attended = jnp.transpose(attended, (2, 0, 1, 3)).reshape(local_rows, kv_local * group_size * HD)
    mixed = lax.psum_scatter(
        jnp.dot(attended, out_weight, preferred_element_type=jnp.float32).astype(jnp.bfloat16),
        "ch",
        scatter_dimension=1,
        tiled=True,
    ).astype(jnp.float32)
    return (hidden + mixed).astype(jnp.bfloat16)


def solution(mesh):
    return jax.shard_map(
        local,
        mesh=mesh,
        in_specs=(
            P(("grp", "seq"), "ch"),
            P(None, "ch"),
            P(None, None, "ch"),
            P(None, "ch", None),
            P("ch"),
            P(None, "ch"),
            P(None, None, "ch"),
            P("ch", None),
        ),
        out_specs=P(("grp", "seq"), "ch"),
        check_vma=False,
    )
```

profile of v0, /device:TPU:0, one launch (start us, length us, event | category | flops | bytes accessed | tf_op | source)
XLA Modules:
  0.0 192.6 jit_solution(12931244962817168558)
XLA Ops:
  6.5 0.0 copy-start
  6.5 0.0 reduce-scatter.4.cloned.1.call-start
  6.5 1.2 fusion.83
  7.8 4.9 %collective-permute-start = (bf16[192,768]{1,0:T(8,128)(2,1)S(1)}, bf16[192,768]{1,0:T(8,128)(2,1)S(1)}, u32[]{:S(2)}, u32[]{:S(2)}) collective-permute-start(bf16[192,768]{1,0:T(8,128)(2,1)S(1)} %get-tuple-element.115), channel_id=1, source_target_pairs={{0,2},{2,4},{4,6},{6,8},{8,10},{10,12},{12,14},{1,3},{3,5},{5,7},{... | collective-permute-start | bytes 884744 | tf_op jit(solution)/shard_map/ppermute | solution.py:18
  12.7 1.3 collective-permute-start.1
  14.0 0.8 slice_reduce_fusion.5
  14.8 0.9 slice_reduce_fusion.4
  15.7 9.5 %collective-permute-done = bf16[192,768]{1,0:T(8,128)(2,1)S(1)} collective-permute-done((bf16[192,768]{1,0:T(8,128)(2,1)S(1)}, bf16[192,768]{1,0:T(8,128)(2,1)S(1)}, u32[]{:S(2)}, u32[]{:S(2)}) %collective-permute-start) | collective-permute-done | bytes 294944 | tf_op jit(solution)/shard_map/ppermute | solution.py:18
  25.2 0.0 collective-permute-done.1
  25.2 1.3 multiply_reduce_fusion
  26.5 2.5 %psum.21 = f32[640]{0:T(1024)S(1)} all-reduce(f32[640]{0:T(1024)S(1)} %multiply_reduce_fusion), channel_id=1, replica_groups=mesh['grp'=2,'seq'=8,'ch'=2] {'ch'}, use_global_device_ids=true, to_apply=%region_1.0 | all-reduce | flops 640 | bytes 5120 | tf_op jit(solution)/shard_map/psum | solution.py:26
  29.0 0.0 copy-done.2
  29.0 0.3 multiply_multiply_fusion.1
  29.2 5.3 %fusion.20 = f32[512,1536]{1,0:T(8,128)} fusion(bf16[2,768,1536]{2,1,0:T(8,128)(2,1)} %param.13, f32[640,768]{1,0:T(8,128)S(1)} %multiply_multiply_fusion.1, f32[768]{0:T(1024)S(1)} %get-tuple-element.86, f32[768]{0:T(1024)S(1)} %get-tuple-element.87, f32[768]{0:T(1024)S(1)} %get-tuple-element.88, f32[768]{0:T(1024)S(1)} %get-tuple-element.89, ...), kind=kOutput, calls=%fused_computation.29 | convolution fusion | flops 1215037440 | bytes 13389824 | tf_op jit(solution)/shard_map/dot_general | solution.py:42
  34.5 0.0 reduce-scatter.4.cloned.1.call-update
  34.6 0.0 reduce-scatter.6.cloned.1.call-start
  34.6 1.4 maximum_convert_fusion
  36.1 11.7 %reduce-scatter.4.cloned.1.call-done = f32[512,768]{1,0:T(8,128)} async-done(((f32[512,1536]{1,0:T(8,128)}), f32[512,768]{1,0:T(8,128)}) %reduce-scatter.4.cloned.1.call-update) | async-done | bytes 1572880 | tf_op jit(solution)/shard_map/reduce_scatter | solution.py:41
  47.8 2.2 %multiply_reduce_fusion.1 = (f32[512]{0:T(512)S(1)}, f32[512,768]{1,0:T(8,128)S(1)}) fusion(f32[512,768]{1,0:T(8,128)} %reduce-scatter.4.cloned.1.call-done, f32[640,768]{1,0:T(8,128)} %maximum_convert_fusion, pred[512]{0:T(512)(128)(4,1)S(1)} %fusion.73), kind=kLoop, calls=%fused_computation.55 | loop fusion | flops 1572352 | bytes 4721152 | tf_op jit(solution)/shard_map/reduce_sum | solution.py:26
  50.0 2.5 %psum.22 = f32[512]{0:T(512)S(1)} all-reduce(f32[512]{0:T(512)S(1)} %get-tuple-element.111), channel_id=1, replica_groups=mesh['grp'=2,'seq'=8,'ch'=2] {'ch'}, use_global_device_ids=true, to_apply=%region_4.5 | all-reduce | flops 512 | bytes 4096 | tf_op jit(solution)/shard_map/psum | solution.py:26
  52.5 0.2 multiply_multiply_fusion.2
  52.7 3.9 %fusion.18 = f32[256,1536]{1,0:T(8,128)} fusion(bf16[2,768,1536]{2,1,0:T(8,128)(2,1)} %param.13, f32[512,768]{1,0:T(8,128)S(1)} %multiply_multiply_fusion.2, f32[768]{0:T(1024)S(1)} %get-tuple-element.91, f32[768]{0:T(1024)S(1)} %get-tuple-element.92, f32[768]{0:T(1024)S(1)} %get-tuple-element.84, f32[768]{0:T(1024)S(1)} %get-tuple-element.85, ...), kind=kOutput, calls=%fused_computation.27 | convolution fusion | flops 607518720 | bytes 7884800 | tf_op jit(solution)/shard_map/dot_general | solution.py:42
  56.6 0.0 copy-start.3
  56.6 0.0 reduce-scatter.6.cloned.1.call-update
  56.6 0.0 reduce-scatter.8.cloned.1.call-start
  56.7 10.3 %reduce-scatter.6.cloned.1.call-done = f32[256,768]{1,0:T(8,128)} async-done(((f32[256,1536]{1,0:T(8,128)}), f32[256,768]{1,0:T(8,128)}) %reduce-scatter.6.cloned.1.call-update) | async-done | bytes 786448 | tf_op jit(solution)/shard_map/reduce_scatter | solution.py:41
  67.0 1.3 multiply_reduce_fusion.2
  68.3 2.5 %psum.23 = f32[256]{0:T(256)S(1)} all-reduce(f32[256]{0:T(256)S(1)} %multiply_reduce_fusion.2), channel_id=1, replica_groups=mesh['grp'=2,'seq'=8,'ch'=2] {'ch'}, use_global_device_ids=true, to_apply=%region_7.8 | all-reduce | flops 256 | bytes 2048 | tf_op jit(solution)/shard_map/psum | solution.py:26
  70.8 0.0 copy-done.3
  70.8 0.0 copy-start.5
  70.8 1.3 multiply_convert_fusion
  72.1 2.4 %all_gather.9 = bf16[256,1536]{1,0:T(8,128)(2,1)S(1)} all-gather(bf16[256,768]{1,0:T(8,128)(2,1)S(1)} %multiply_convert_fusion), channel_id=1, replica_groups=mesh['grp'=2,'seq'=8,'ch'=2] {'ch'}, dimensions={1}, use_global_device_ids=true | all-gather | bytes 1179648 | tf_op jit(solution)/shard_map/all_gather | solution.py:77
  74.5 0.0 copy-done.5
  74.5 0.4 convolution_convert_fusion.2
  74.9 33.7 %all_gather.10 = bf16[2048,128]{1,0:T(8,128)(2,1)} all-gather(bf16[256,128]{1,0:T(8,128)(2,1)S(1)} %get-tuple-element.118), channel_id=1, replica_groups=mesh['grp'=2,'seq'=8,'ch'=2] {'seq'}, dimensions={0}, use_global_device_ids=true | all-gather | bytes 589824 | tf_op jit(solution)/shard_map/all_gather | solution.py:120
  108.6 33.4 %all_gather.11 = bf16[2048,128]{1,0:T(8,128)(2,1)} all-gather(bf16[256,128]{1,0:T(8,128)(2,1)S(1)} %get-tuple-element.117), channel_id=1, replica_groups=mesh['grp'=2,'seq'=8,'ch'=2] {'seq'}, dimensions={0}, use_global_device_ids=true | all-gather | bytes 589824 | tf_op jit(solution)/shard_map/all_gather | solution.py:121
  142.0 0.0 copy-done.4
  142.0 0.6 convolution_convert_fusion.1
  142.6 0.8 reshape.86
  143.3 1.0 copy.15
  144.3 25.2 %while.15 = (s32[]{:T(128)}, f32[1,4,256]{2,1,0:T(4,128)S(1)}, f32[1,4,256]{2,1,0:T(4,128)S(1)}, f32[1,4,256,128]{3,2,1,0:T(8,128)}, bf16[4,512,1,128]{3,1,2,0:T...) while((s32[]{:T(128)}, f32[1,4,256]{2,1,0:T(4,128)S(1)}, ...), condition=%wide.region_11.12_spmd.clone, body=%wide.region_8.11_spmd.clone.sunk | while | flops 273029120 | bytes 16319621 | solution.py:128
  144.3 2.7 %bitcast_reduce_fusion.2 = (f32[4,256]{1,0:T(4,128)S(1)}, f32[512,256,4]{1,0,2:T(8,128)}) fusion(bf16[256,1,4,128]{3,0,2,1:T(8,128)(2,1)S(1)} %get-tuple-element.193, bf16[4,512,1,128]{3,1,2,0:T(8,128)(2,1)} %get-tuple-element.192, s32[]{:T(128)} %get-tuple-element.179), kind=kOutput, calls=%fused_computation.1.clone.1 | convolution fusion | flops 135265280 | bytes 2494976 | tf_op jit(solution)/shard_map/while/body/eval_jaxpr/pkgd,skd->kgps/dot_general | solution.py:98
  147.1 3.1 %fusion.99 = f32[1,4,256,128]{3,2,1,0:T(8,128)} fusion(f32[512,256,4]{1,0,2:T(8,128)} %get-tuple-element.168, f32[4,256]{1,0:T(4,128)S(1)} %bitcast.95, f32[1,4,256,128]{3,2,1,0:T(8,128)} %get-tuple-element.182, f32[4,256]{1,0:T(4,128)S(1)} %get-tuple-element.169, pred[]{:T(512)S(6)} %compare.3, bf16[4,512,1,128]{3,1,2,0:T(8,128)(2,1)} %get-tuple-element.194, ...), kind=kOutput, calls=%fused_computation.6.clone.1 | convolution fusion | flops 136183808 | bytes 3285505 | tf_op jit(solution)/shard_map/while/body/eval_jaxpr/kgps,skd->kgpd/dot_general | solution.py:105
  150.1 0.0 copy-done.1
  150.1 0.4 fusion.98
  150.5 2.7 %bitcast_reduce_fusion.2 = (f32[4,256]{1,0:T(4,128)S(1)}, f32[512,256,4]{1,0,2:T(8,128)}) fusion(bf16[256,1,4,128]{3,0,2,1:T(8,128)(2,1)S(1)} %get-tuple-element.193, bf16[4,512,1,128]{3,1,2,0:T(8,128)(2,1)} %get-tuple-element.192, s32[]{:T(128)} %get-tuple-element.179), kind=kOutput, calls=%fused_computation.1.clone.1 | convolution fusion | flops 135265280 | bytes 2494976 | tf_op jit(solution)/shard_map/while/body/eval_jaxpr/pkgd,skd->kgps/dot_general | solution.py:98
  153.3 3.2 %fusion.99 = f32[1,4,256,128]{3,2,1,0:T(8,128)} fusion(f32[512,256,4]{1,0,2:T(8,128)} %get-tuple-element.168, f32[4,256]{1,0:T(4,128)S(1)} %bitcast.95, f32[1,4,256,128]{3,2,1,0:T(8,128)} %get-tuple-element.182, f32[4,256]{1,0:T(4,128)S(1)} %get-tuple-element.169, pred[]{:T(512)S(6)} %compare.3, bf16[4,512,1,128]{3,1,2,0:T(8,128)(2,1)} %get-tuple-element.194, ...), kind=kOutput, calls=%fused_computation.6.clone.1 | convolution fusion | flops 136183808 | bytes 3285505 | tf_op jit(solution)/shard_map/while/body/eval_jaxpr/kgps,skd->kgpd/dot_general | solution.py:105
  156.5 0.0 copy-done.1
  156.5 0.4 fusion.98
  156.9 2.7 %bitcast_reduce_fusion.2 = (f32[4,256]{1,0:T(4,128)S(1)}, f32[512,256,4]{1,0,2:T(8,128)}) fusion(bf16[256,1,4,128]{3,0,2,1:T(8,128)(2,1)S(1)} %get-tuple-element.193, bf16[4,512,1,128]{3,1,2,0:T(8,128)(2,1)} %get-tuple-element.192, s32[]{:T(128)} %get-tuple-element.179), kind=kOutput, calls=%fused_computation.1.clone.1 | convolution fusion | flops 135265280 | bytes 2494976 | tf_op jit(solution)/shard_map/while/body/eval_jaxpr/pkgd,skd->kgps/dot_general | solution.py:98
  159.6 3.2 %fusion.99 = f32[1,4,256,128]{3,2,1,0:T(8,128)} fusion(f32[512,256,4]{1,0,2:T(8,128)} %get-tuple-element.168, f32[4,256]{1,0:T(4,128)S(1)} %bitcast.95, f32[1,4,256,128]{3,2,1,0:T(8,128)} %get-tuple-element.182, f32[4,256]{1,0:T(4,128)S(1)} %get-tuple-element.169, pred[]{:T(512)S(6)} %compare.3, bf16[4,512,1,128]{3,1,2,0:T(8,128)(2,1)} %get-tuple-element.194, ...), kind=kOutput, calls=%fused_computation.6.clone.1 | convolution fusion | flops 136183808 | bytes 3285505 | tf_op jit(solution)/shard_map/while/body/eval_jaxpr/kgps,skd->kgpd/dot_general | solution.py:105
  162.8 0.0 copy-done.1
  162.8 0.4 fusion.98
  163.2 2.7 %bitcast_reduce_fusion.2 = (f32[4,256]{1,0:T(4,128)S(1)}, f32[512,256,4]{1,0,2:T(8,128)}) fusion(bf16[256,1,4,128]{3,0,2,1:T(8,128)(2,1)S(1)} %get-tuple-element.193, bf16[4,512,1,128]{3,1,2,0:T(8,128)(2,1)} %get-tuple-element.192, s32[]{:T(128)} %get-tuple-element.179), kind=kOutput, calls=%fused_computation.1.clone.1 | convolution fusion | flops 135265280 | bytes 2494976 | tf_op jit(solution)/shard_map/while/body/eval_jaxpr/pkgd,skd->kgps/dot_general | solution.py:98
  165.9 3.2 %fusion.99 = f32[1,4,256,128]{3,2,1,0:T(8,128)} fusion(f32[512,256,4]{1,0,2:T(8,128)} %get-tuple-element.168, f32[4,256]{1,0:T(4,128)S(1)} %bitcast.95, f32[1,4,256,128]{3,2,1,0:T(8,128)} %get-tuple-element.182, f32[4,256]{1,0:T(4,128)S(1)} %get-tuple-element.169, pred[]{:T(512)S(6)} %compare.3, bf16[4,512,1,128]{3,1,2,0:T(8,128)(2,1)} %get-tuple-element.194, ...), kind=kOutput, calls=%fused_computation.6.clone.1 | convolution fusion | flops 136183808 | bytes 3285505 | tf_op jit(solution)/shard_map/while/body/eval_jaxpr/kgps,skd->kgpd/dot_general | solution.py:105
  169.1 0.0 copy-done.1
  169.1 0.4 fusion.98
  169.5 2.1 %copy.17 = f32[1,4,256,128]{2,3,1,0:T(8,128)} copy(f32[1,4,256,128]{3,2,1,0:T(8,128)} %get-tuple-element.43) | data formatting | bytes 1048576 | tf_op jit(solution)/shard_map/while | solution.py:128
  171.6 1.1 divide_convert_fusion
  172.7 0.0 copy-done
  172.7 1.5 convolution_convert_fusion
  174.2 0.0 reduce-scatter.8.cloned.1.call-update
  174.2 9.8 %reduce-scatter.8.cloned.1.call-done = bf16[256,768]{1,0:T(8,128)(2,1)} async-done(((bf16[256,1536]{1,0:T(8,128)(2,1)}), bf16[256,768]{1,0:T(8,128)(2,1)}) %reduce-scatter.8.cloned.1.call-update) | async-done | bytes 393232 | tf_op jit(solution)/shard_map/reduce_scatter | solution.py:132
  184.0 2.1 %add_convert_fusion = bf16[256,768]{1,0:T(8,128)(2,1)} fusion(bf16[256,768]{1,0:T(8,128)(2,1)} %reduce-scatter.8.cloned.1.call-done, f32[256,768]{1,0:T(8,128)} %reduce-scatter.6.cloned.1.call-done, f32[512,768]{1,0:T(8,128)S(1)} %get-tuple-element.112), kind=kLoop, calls=%fused_computation.80 | loop fusion | flops 786432 | bytes 2359296 | tf_op jit(solution)/shard_map/convert_element_type | solution.py:138
  (26 shorter events, 0.2 us)
Async XLA Ops:
  6.5 166.2 %copy-start = (bf16[512,1536]{1,0:T(8,128)(2,1)S(1)}, bf16[512,1536]{1,0:T(8,128)(2,1)}, u32[]{:S(2)}) copy-start(bf16[512,1536]{1,0:T(8,128)(2,1)} %param.17) | copy-start | bytes 4718596
  6.5 22.4 %copy-start.2 = (bf16[256,768]{1,0:T(8,128)(2,1)S(1)}, bf16[256,768]{1,0:T(8,128)(2,1)}, u32[]{:S(2)}) copy-start(bf16[256,768]{1,0:T(8,128)(2,1)} %param.10) | copy-start | bytes 1179652
  6.5 41.2 %reduce-scatter.4.cloned.1.call-start = ((), (), s32[]{:S(2)}) async-start(), calls=%async_computation.3 | async-start | bytes 4718592 | tf_op jit(solution)/shard_map/reduce_scatter | solution.py:41
  7.8 17.4 %collective-permute-start = (bf16[192,768]{1,0:T(8,128)(2,1)S(1)}, bf16[192,768]{1,0:T(8,128)(2,1)S(1)}, u32[]{:S(2)}, u32[]{:S(2)}) collective-permute-start(bf16[192,768]{1,0:T(8,128)(2,1)S(1)} %get-tuple-element.115), channel_id=1, source_target_pairs={{0,2},{2,4},{4,6},{6,8},{8,10},{10,12},{12,14},{1,3},{3,5},{5,7},{... | collective-permute-start | bytes 884744 | tf_op jit(solution)/shard_map/ppermute | solution.py:18
  12.7 12.6 %collective-permute-start.1 = (bf16[192,768]{1,0:T(8,128)(2,1)S(1)}, bf16[192,768]{1,0:T(8,128)(2,1)S(1)}, u32[]{:S(2)}, u32[]{:S(2)}) collective-permute-start(bf16[192,768]{1,0:T(8,128)(2,1)S(1)} %get-tuple-element.116), channel_id=1, source_target_pairs={{2,0},{4,2},{6,4},{8,6},{10,8},{12,10},{14,12},{3,1},{5,3},{7,5},{... | collective-permute-start | bytes 884744 | tf_op jit(solution)/shard_map/ppermute | solution.py:19
  34.6 32.4 %reduce-scatter.6.cloned.1.call-start = ((), (), s32[]{:S(2)}) async-start(), calls=%async_computation.4 | async-start | bytes 2359296 | tf_op jit(solution)/shard_map/reduce_scatter | solution.py:41
  56.6 14.2 %copy-start.3 = (f32[768]{0:T(1024)S(1)}, f32[768]{0:T(1024)}, u32[]{:S(2)}) copy-start(f32[768]{0:T(1024)} %param.14) | copy-start | bytes 9220
  56.6 127.4 %reduce-scatter.8.cloned.1.call-start = ((), (), s32[]{:S(2)}) async-start(), calls=%async_computation.5 | async-start | bytes 1179648 | tf_op jit(solution)/shard_map/reduce_scatter | solution.py:132
  70.8 3.7 %copy-start.5 = (bf16[1536,2,128]{2,1,0:T(2,128)(2,1)S(1)}, bf16[1536,2,128]{2,1,0:T(2,128)(2,1)}, u32[]{:S(2)}) copy-start(bf16[1536,2,128]{2,1,0:T(2,128)(2,1)} %param.16) | copy-start | bytes 2359300
  74.5 67.5 %copy-start.4 = (bf16[1536,512]{1,0:T(8,128)(2,1)S(1)}, bf16[1536,512]{1,0:T(8,128)(2,1)}, u32[]{:S(2)}) copy-start(bf16[1536,512]{1,0:T(8,128)(2,1)} %param.15) | copy-start | bytes 4718596
  147.0 3.1 %copy-start.1 = (f32[512,256,4]{1,0,2:T(8,128)S(1)}, f32[512,256,4]{1,0,2:T(8,128)}, u32[]{:S(2)}) copy-start(f32[512,256,4]{1,0,2:T(8,128)} %get-tuple-element.168) | copy-start | bytes 6291460 | tf_op jit(solution)/shard_map/while
  153.3 3.2 %copy-start.1 = (f32[512,256,4]{1,0,2:T(8,128)S(1)}, f32[512,256,4]{1,0,2:T(8,128)}, u32[]{:S(2)}) copy-start(f32[512,256,4]{1,0,2:T(8,128)} %get-tuple-element.168) | copy-start | bytes 6291460 | tf_op jit(solution)/shard_map/while
  159.6 3.2 %copy-start.1 = (f32[512,256,4]{1,0,2:T(8,128)S(1)}, f32[512,256,4]{1,0,2:T(8,128)}, u32[]{:S(2)}) copy-start(f32[512,256,4]{1,0,2:T(8,128)} %get-tuple-element.168) | copy-start | bytes 6291460 | tf_op jit(solution)/shard_map/while
  165.9 3.2 %copy-start.1 = (f32[512,256,4]{1,0,2:T(8,128)S(1)}, f32[512,256,4]{1,0,2:T(8,128)}, u32[]{:S(2)}) copy-start(f32[512,256,4]{1,0,2:T(8,128)} %get-tuple-element.168) | copy-start | bytes 6291460 | tf_op jit(solution)/shard_map/while
Sparse Core Ops, SparseCore 0:
  34.7 13.0 reduce-scatter.3
  56.7 10.2 reduce-scatter.5
  174.3 9.6 reduce-scatter.7
where the time goes:
time: 193 us
  blocking collectives  76.9 us (40%)
  waiting for transfers between devices  41.4 us (21%)
  matrix products  35.1 us (18%)
  between operations  13.2 us (7%)
  other arithmetic  12.8 us (7%)
  local copies, waits for them, and re-layouts  6.81 us (4%)
  starting transfers between devices  6.27 us (3%)
    all_gather x1, blocking collectives, local(): key_piece = lax.all_gather(keys_local, 'seq', axis=0, tiled=True)  33.7 us
    all_gather x1, blocking collectives, local(): value_piece = lax.all_gather(values_local, 'seq', axis=0, tiled=True)  33.4 us
    reduce_scatter x2, waiting for transfers between devices, channel_mix(): lax.psum_scatter(jnp.dot(gelu_output, weight, preferred_element_type=jnp....  22 us
    dot_general x4, matrix products, key_block(): jnp.einsum('kgps,skd->kgpd', probs.astype(jnp.bfloat16), value_part, pref...  12.7 us
    dot_general x4, matrix products, key_block(): jnp.einsum('pkgd,skd->kgps', query_grid, key_part, preferred_element_type...  10.8 us
    reduce_scatter x1, waiting for transfers between devices, local(): lax.psum_scatter(jnp.dot(attended, out_weight, preferred_element_type=jnp...  9.8 us
    ppermute x1, waiting for transfers between devices, extended(): before = lax.ppermute(last, axis, up)  9.54 us
    dot_general x2, matrix products, channel_mix(): jnp.dot(gelu_output, weight, preferred_element_type=jnp.float32)  9.19 us
  transfers between devices with their start and end apart: 5, of which 4 were waited for; matrix products, arithmetic and copies ran while one was open for 2% of the time, Pallas kernels for 0%

commit v1 on v0

--- a/solution.py
+++ b/solution.py
@@ -118,7 +118,12 @@
     )
     carry = initial
     key_piece = lax.all_gather(keys_local, "seq", axis=0, tiled=True)
-    value_piece = lax.all_gather(values_local, "seq", axis=0, tiled=True)
+    ring = [values_local]
+    for hop in range(7):
+        ring.append(lax.ppermute(ring[-1], "seq", [(dev, (dev + 1) % 8) for dev in range(8)]))
+    value_piece = jnp.roll(
+        jnp.concatenate(ring[::-1], axis=0), (lax.axis_index("seq") + 1) * ring[0].shape[0], axis=0
+    )
     key_count = key_piece.shape[0]
     block_len = math.gcd(key_count, 512)
     blocks = (

time: 193 us -> 217 us (1.12)
  waiting for transfers between devices: 41.4 us -> 82.6 us
  blocking collectives: 76.9 us -> 43.1 us
  local copies, waits for them, and re-layouts: 6.81 us -> 18.8 us
    ppermute x0 -> x7, waiting for transfers between devices: none -> 44 us  [local(): lax.ppermute(ring[-1], 'seq', [(dev, (dev + 1) % 8) for dev in range(8)])]
    all_gather x1 -> x0, blocking collectives: 33.4 us -> none  [local(): value_piece = lax.all_gather(values_local, 'seq', axis=0, tiled=True)]
    unnamed x11 -> x46, local copies, waits for them, and re-layouts: 1 us -> 12.2 us
    reduce_scatter x1, waiting for transfers between devices: 9.8 us -> 6.97 us  [local(): lax.psum_scatter(jnp.dot(attended, out_weight, preferred_element_type=jnp...]
  transfers between devices with their start and end apart: 5 -> 12, of which waited for: 4 -> 11; matrix products, arithmetic and copies ran while one was open for 2% -> 3% of each run, Pallas kernels for 0% -> 0%
where the time goes in v1:
time: 217 us; the launch traced here: 216 us
  waiting for transfers between devices  82.6 us (38%)
  blocking collectives  43.1 us (20%)
  matrix products  36.7 us (17%)
  local copies, waits for them, and re-layouts  18.8 us (9%)
  between operations  13.3 us (6%)
  other arithmetic  12.8 us (6%)
  starting transfers between devices  8.09 us (4%)
    ppermute x7, waiting for transfers between devices, local(): lax.ppermute(ring[-1], 'seq', [(dev, (dev + 1) % 8) for dev in range(8)])  44 us
    all_gather x1, blocking collectives, local(): key_piece = lax.all_gather(keys_local, 'seq', axis=0, tiled=True)  33.3 us
    reduce_scatter x2, waiting for transfers between devices, channel_mix(): lax.psum_scatter(jnp.dot(gelu_output, weight, preferred_element_type=jnp....  22 us
    dot_general x4, matrix products, key_block(): jnp.einsum('kgps,skd->kgpd', probs.astype(jnp.bfloat16), value_part, pref...  12.7 us
    unnamed x46, local copies, waits for them, and re-layouts  12.2 us
    dot_general x4, matrix products, key_block(): jnp.einsum('pkgd,skd->kgps', query_grid, key_part, preferred_element_type...  10.8 us
    ppermute x1, waiting for transfers between devices, extended(): before = lax.ppermute(last, axis, up)  9.54 us
    dot_general x2, matrix products, channel_mix(): jnp.dot(gelu_output, weight, preferred_element_type=jnp.float32)  9.19 us
  transfers between devices with their start and end apart: 12, of which 11 were waited for; matrix products, arithmetic and copies ran while one was open for 3% of the time, Pallas kernels for 0%

profile of v1, /device:TPU:0, one launch (start us, length us, event | category | flops | bytes accessed | tf_op | source)
XLA Modules:
  0.0 215.6 jit_solution(14444836839319954009)
XLA Ops:
  6.5 1.2 fusion.83
  7.8 4.9 %collective-permute-start = (bf16[192,768]{1,0:T(8,128)(2,1)S(1)}, bf16[192,768]{1,0:T(8,128)(2,1)S(1)}, u32[]{:S(2)}, u32[]{:S(2)}) collective-permute-start(bf16[192,768]{1,0:T(8,128)(2,1)S(1)} %get-tuple-element.115), channel_id=1, source_target_pairs={{0,2},{2,4},{4,6},{6,8},{8,10},{10,12},{12,14},{1,3},{3,5},{5,7},{... | collective-permute-start | bytes 884744 | tf_op jit(solution)/shard_map/ppermute | solution.py:18
  12.7 1.3 collective-permute-start.1
  14.0 0.8 slice_reduce_fusion.5
  14.8 0.9 slice_reduce_fusion.4
  15.7 9.5 %collective-permute-done = bf16[192,768]{1,0:T(8,128)(2,1)S(1)} collective-permute-done((bf16[192,768]{1,0:T(8,128)(2,1)S(1)}, bf16[192,768]{1,0:T(8,128)(2,1)S(1)}, u32[]{:S(2)}, u32[]{:S(2)}) %collective-permute-start) | collective-permute-done | bytes 294944 | tf_op jit(solution)/shard_map/ppermute | solution.py:18
  25.2 1.3 multiply_reduce_fusion
  26.5 2.5 %psum.21 = f32[640]{0:T(1024)S(1)} all-reduce(f32[640]{0:T(1024)S(1)} %multiply_reduce_fusion), channel_id=1, replica_groups=mesh['grp'=2,'seq'=8,'ch'=2] {'ch'}, use_global_device_ids=true, to_apply=%region_1.0 | all-reduce | flops 640 | bytes 5120 | tf_op jit(solution)/shard_map/psum | solution.py:26
  29.2 5.3 %fusion.20 = f32[512,1536]{1,0:T(8,128)} fusion(bf16[2,768,1536]{2,1,0:T(8,128)(2,1)} %param.13, f32[640,768]{1,0:T(8,128)S(1)} %multiply_multiply_fusion.1, f32[768]{0:T(1024)S(1)} %get-tuple-element.86, f32[768]{0:T(1024)S(1)} %get-tuple-element.87, f32[768]{0:T(1024)S(1)} %get-tuple-element.88, f32[768]{0:T(1024)S(1)} %get-tuple-element.89, ...), kind=kOutput, calls=%fused_computation.29 | convolution fusion | flops 1215037440 | bytes 13389824 | tf_op jit(solution)/shard_map/dot_general | solution.py:42
  34.6 1.4 maximum_convert_fusion
  36.1 11.7 %reduce-scatter.4.cloned.1.call-done = f32[512,768]{1,0:T(8,128)} async-done(((f32[512,1536]{1,0:T(8,128)}), f32[512,768]{1,0:T(8,128)}) %reduce-scatter.4.cloned.1.call-update) | async-done | bytes 1572880 | tf_op jit(solution)/shard_map/reduce_scatter | solution.py:41
  47.8 2.2 %multiply_reduce_fusion.1 = (f32[512]{0:T(512)S(1)}, f32[512,768]{1,0:T(8,128)S(1)}) fusion(f32[512,768]{1,0:T(8,128)} %reduce-scatter.4.cloned.1.call-done, f32[640,768]{1,0:T(8,128)} %maximum_convert_fusion, pred[512]{0:T(512)(128)(4,1)S(1)} %fusion.73), kind=kLoop, calls=%fused_computation.55 | loop fusion | flops 1572352 | bytes 4721152 | tf_op jit(solution)/shard_map/reduce_sum | solution.py:26
  50.0 2.5 %psum.22 = f32[512]{0:T(512)S(1)} all-reduce(f32[512]{0:T(512)S(1)} %get-tuple-element.111), channel_id=1, replica_groups=mesh['grp'=2,'seq'=8,'ch'=2] {'ch'}, use_global_device_ids=true, to_apply=%region_4.5 | all-reduce | flops 512 | bytes 4096 | tf_op jit(solution)/shard_map/psum | solution.py:26
  52.7 3.9 %fusion.18 = f32[256,1536]{1,0:T(8,128)} fusion(bf16[2,768,1536]{2,1,0:T(8,128)(2,1)} %param.13, f32[512,768]{1,0:T(8,128)S(1)} %multiply_multiply_fusion.2, f32[768]{0:T(1024)S(1)} %get-tuple-element.91, f32[768]{0:T(1024)S(1)} %get-tuple-element.92, f32[768]{0:T(1024)S(1)} %get-tuple-element.84, f32[768]{0:T(1024)S(1)} %get-tuple-element.85, ...), kind=kOutput, calls=%fused_computation.27 | convolution fusion | flops 607518720 | bytes 7884800 | tf_op jit(solution)/shard_map/dot_general | solution.py:42
  56.7 10.3 %reduce-scatter.6.cloned.1.call-done = f32[256,768]{1,0:T(8,128)} async-done(((f32[256,1536]{1,0:T(8,128)}), f32[256,768]{1,0:T(8,128)}) %reduce-scatter.6.cloned.1.call-update) | async-done | bytes 786448 | tf_op jit(solution)/shard_map/reduce_scatter | solution.py:41
  67.0 1.3 multiply_reduce_fusion.2
  68.3 2.5 %psum.23 = f32[256]{0:T(256)S(1)} all-reduce(f32[256]{0:T(256)S(1)} %multiply_reduce_fusion.2), channel_id=1, replica_groups=mesh['grp'=2,'seq'=8,'ch'=2] {'ch'}, use_global_device_ids=true, to_apply=%region_7.8 | all-reduce | flops 256 | bytes 2048 | tf_op jit(solution)/shard_map/psum | solution.py:26
  70.8 1.3 multiply_convert_fusion
  72.1 2.4 %all_gather.6 = bf16[256,1536]{1,0:T(8,128)(2,1)S(1)} all-gather(bf16[256,768]{1,0:T(8,128)(2,1)S(1)} %multiply_convert_fusion), channel_id=1, replica_groups=mesh['grp'=2,'seq'=8,'ch'=2] {'ch'}, dimensions={1}, use_global_device_ids=true | all-gather | bytes 1179648 | tf_op jit(solution)/shard_map/all_gather | solution.py:77
  74.5 0.9 copy-done.3
  75.4 0.4 convolution_convert_fusion.2
  75.8 1.8 collective-permute-start.2
  77.6 5.3 %collective-permute-done.2 = bf16[256,128]{1,0:T(8,128)(2,1)S(1)} collective-permute-done((bf16[256,128]{1,0:T(8,128)(2,1)S(1)}, bf16[256,128]{1,0:T(8,128)(2,1)S(1)}, u32[]{:S(2)}, u32[]{:S(2)}) %collective-permute-start.2) | collective-permute-done | bytes 65568 | tf_op jit(solution)/shard_map/ppermute | solution.py:123
  82.9 0.6 copy-done.4
  83.5 7.0 %collective-permute-done.3 = bf16[256,128]{1,0:T(8,128)(2,1)S(1)} collective-permute-done((bf16[256,128]{1,0:T(8,128)(2,1)S(1)}, bf16[256,128]{1,0:T(8,128)(2,1)S(1)}, u32[]{:S(2)}, u32[]{:S(2)}) %collective-permute-start.3) | collective-permute-done | bytes 65568 | tf_op jit(solution)/shard_map/ppermute | solution.py:123
  90.5 0.6 copy-done.6
  91.1 7.0 %collective-permute-done.4 = bf16[256,128]{1,0:T(8,128)(2,1)S(1)} collective-permute-done((bf16[256,128]{1,0:T(8,128)(2,1)S(1)}, bf16[256,128]{1,0:T(8,128)(2,1)S(1)}, u32[]{:S(2)}, u32[]{:S(2)}) %collective-permute-start.4) | collective-permute-done | bytes 65568 | tf_op jit(solution)/shard_map/ppermute | solution.py:123
  98.1 0.6 copy-done.8
  98.7 7.0 %collective-permute-done.5 = bf16[256,128]{1,0:T(8,128)(2,1)S(1)} collective-permute-done((bf16[256,128]{1,0:T(8,128)(2,1)S(1)}, bf16[256,128]{1,0:T(8,128)(2,1)S(1)}, u32[]{:S(2)}, u32[]{:S(2)}) %collective-permute-start.5) | collective-permute-done | bytes 65568 | tf_op jit(solution)/shard_map/ppermute | solution.py:123
  105.6 0.6 copy-done.10
  106.3 7.0 %collective-permute-done.6 = bf16[256,128]{1,0:T(8,128)(2,1)S(1)} collective-permute-done((bf16[256,128]{1,0:T(8,128)(2,1)S(1)}, bf16[256,128]{1,0:T(8,128)(2,1)S(1)}, u32[]{:S(2)}, u32[]{:S(2)}) %collective-permute-start.6) | collective-permute-done | bytes 65568 | tf_op jit(solution)/shard_map/ppermute | solution.py:123
  113.2 7.6 %collective-permute-done.7 = bf16[256,128]{1,0:T(8,128)(2,1)} collective-permute-done((bf16[256,128]{1,0:T(8,128)(2,1)S(1)}, bf16[256,128]{1,0:T(8,128)(2,1)}, u32[]{:S(2)}, u32[]{:S(2)}) %collective-permute-start.7) | collective-permute-done | bytes 65568 | tf_op jit(solution)/shard_map/ppermute | solution.py:123
  120.8 2.2 %convolution_convert_fusion.1 = bf16[256,512]{1,0:T(8,128)(2,1)S(1)} fusion(bf16[256,1536]{1,0:T(8,128)(2,1)} %copy-done.3, bf16[1536,512]{1,0:T(8,128)(2,1)} %param.15), kind=kOutput, calls=%fused_computation.56 | convolution fusion | flops 402784256 | bytes 2621440 | tf_op jit(solution)/shard_map/dot_general | solution.py:78
  123.1 0.8 reshape.86
  123.9 1.0 copy.14
  124.9 3.2 %collective-permute-done.8 = bf16[256,128]{1,0:T(8,128)(2,1)} collective-permute-done((bf16[256,128]{1,0:T(8,128)(2,1)}, bf16[256,128]{1,0:T(8,128)(2,1)}, u32[]{:S(2)}, u32[]{:S(2)}) %collective-permute-start.8) | collective-permute-done | bytes 65568 | tf_op jit(solution)/shard_map/ppermute | solution.py:123
  128.1 0.8 constant_dynamic-update-slice_fusion.15
  129.0 0.9 constant_dynamic-update-slice_fusion.14
  129.8 0.9 constant_dynamic-update-slice_fusion.13
  130.7 0.9 constant_dynamic-update-slice_fusion.12
  131.5 0.9 constant_dynamic-update-slice_fusion.11
  132.4 0.9 constant_dynamic-update-slice_fusion.10
  133.2 0.9 constant_dynamic-update-slice_fusion.9
  134.1 0.9 constant_dynamic-update-slice_fusion.7
  135.0 0.9 constant_dynamic-update-slice_fusion.6
  136.0 33.3 %all_gather.7 = bf16[2048,128]{1,0:T(8,128)(2,1)} all-gather(bf16[256,128]{1,0:T(8,128)(2,1)S(1)} %get-tuple-element.118), channel_id=1, replica_groups=mesh['grp'=2,'seq'=8,'ch'=2] {'seq'}, dimensions={0}, use_global_device_ids=true | all-gather | bytes 589824 | tf_op jit(solution)/shard_map/all_gather | solution.py:120
  169.3 0.8 constant_dynamic-slice_fusion
  170.1 25.2 %while.15 = (s32[]{:T(128)}, f32[1,4,256]{2,1,0:T(4,128)S(1)}, f32[1,4,256]{2,1,0:T(4,128)S(1)}, f32[1,4,256,128]{3,2,1,0:T(8,128)}, bf16[4,512,1,128]{3,1,2,0:T...) while((s32[]{:T(128)}, f32[1,4,256]{2,1,0:T(4,128)S(1)}, ...), condition=%wide.region_11.12_spmd.clone, body=%wide.region_8.11_spmd.clone.sunk | while | flops 273029120 | bytes 16319621 | solution.py:133
  170.1 2.7 %bitcast_reduce_fusion.2 = (f32[4,256]{1,0:T(4,128)S(1)}, f32[512,256,4]{1,0,2:T(8,128)}) fusion(bf16[256,1,4,128]{3,0,2,1:T(8,128)(2,1)S(1)} %get-tuple-element.193, bf16[4,512,1,128]{3,1,2,0:T(8,128)(2,1)} %get-tuple-element.192, s32[]{:T(128)} %get-tuple-element.179), kind=kOutput, calls=%fused_computation.1.clone.1 | convolution fusion | flops 135265280 | bytes 2494976 | tf_op jit(solution)/shard_map/while/body/eval_jaxpr/pkgd,skd->kgps/dot_general | solution.py:98
  172.8 3.1 %fusion.98 = f32[1,4,256,128]{3,2,1,0:T(8,128)} fusion(f32[512,256,4]{1,0,2:T(8,128)} %get-tuple-element.168, f32[4,256]{1,0:T(4,128)S(1)} %bitcast.93, f32[1,4,256,128]{3,2,1,0:T(8,128)} %get-tuple-element.182, f32[4,256]{1,0:T(4,128)S(1)} %get-tuple-element.169, pred[]{:T(512)S(6)} %compare.4, bf16[4,512,1,128]{3,1,2,0:T(8,128)(2,1)} %get-tuple-element.194, ...), kind=kOutput, calls=%fused_computation.6.clone.1 | convolution fusion | flops 136183808 | bytes 3285505 | tf_op jit(solution)/shard_map/while/body/eval_jaxpr/kgps,skd->kgpd/dot_general | solution.py:105
  175.9 0.4 fusion.97
  176.3 2.7 %bitcast_reduce_fusion.2 = (f32[4,256]{1,0:T(4,128)S(1)}, f32[512,256,4]{1,0,2:T(8,128)}) fusion(bf16[256,1,4,128]{3,0,2,1:T(8,128)(2,1)S(1)} %get-tuple-element.193, bf16[4,512,1,128]{3,1,2,0:T(8,128)(2,1)} %get-tuple-element.192, s32[]{:T(128)} %get-tuple-element.179), kind=kOutput, calls=%fused_computation.1.clone.1 | convolution fusion | flops 135265280 | bytes 2494976 | tf_op jit(solution)/shard_map/while/body/eval_jaxpr/pkgd,skd->kgps/dot_general | solution.py:98
  179.0 3.2 %fusion.98 = f32[1,4,256,128]{3,2,1,0:T(8,128)} fusion(f32[512,256,4]{1,0,2:T(8,128)} %get-tuple-element.168, f32[4,256]{1,0:T(4,128)S(1)} %bitcast.93, f32[1,4,256,128]{3,2,1,0:T(8,128)} %get-tuple-element.182, f32[4,256]{1,0:T(4,128)S(1)} %get-tuple-element.169, pred[]{:T(512)S(6)} %compare.4, bf16[4,512,1,128]{3,1,2,0:T(8,128)(2,1)} %get-tuple-element.194, ...), kind=kOutput, calls=%fused_computation.6.clone.1 | convolution fusion | flops 136183808 | bytes 3285505 | tf_op jit(solution)/shard_map/while/body/eval_jaxpr/kgps,skd->kgpd/dot_general | solution.py:105
  182.2 0.4 fusion.97
  182.6 2.7 %bitcast_reduce_fusion.2 = (f32[4,256]{1,0:T(4,128)S(1)}, f32[512,256,4]{1,0,2:T(8,128)}) fusion(bf16[256,1,4,128]{3,0,2,1:T(8,128)(2,1)S(1)} %get-tuple-element.193, bf16[4,512,1,128]{3,1,2,0:T(8,128)(2,1)} %get-tuple-element.192, s32[]{:T(128)} %get-tuple-element.179), kind=kOutput, calls=%fused_computation.1.clone.1 | convolution fusion | flops 135265280 | bytes 2494976 | tf_op jit(solution)/shard_map/while/body/eval_jaxpr/pkgd,skd->kgps/dot_general | solution.py:98
  185.4 3.2 %fusion.98 = f32[1,4,256,128]{3,2,1,0:T(8,128)} fusion(f32[512,256,4]{1,0,2:T(8,128)} %get-tuple-element.168, f32[4,256]{1,0:T(4,128)S(1)} %bitcast.93, f32[1,4,256,128]{3,2,1,0:T(8,128)} %get-tuple-element.182, f32[4,256]{1,0:T(4,128)S(1)} %get-tuple-element.169, pred[]{:T(512)S(6)} %compare.4, bf16[4,512,1,128]{3,1,2,0:T(8,128)(2,1)} %get-tuple-element.194, ...), kind=kOutput, calls=%fused_computation.6.clone.1 | convolution fusion | flops 136183808 | bytes 3285505 | tf_op jit(solution)/shard_map/while/body/eval_jaxpr/kgps,skd->kgpd/dot_general | solution.py:105
  188.6 0.4 fusion.97
  189.0 2.7 %bitcast_reduce_fusion.2 = (f32[4,256]{1,0:T(4,128)S(1)}, f32[512,256,4]{1,0,2:T(8,128)}) fusion(bf16[256,1,4,128]{3,0,2,1:T(8,128)(2,1)S(1)} %get-tuple-element.193, bf16[4,512,1,128]{3,1,2,0:T(8,128)(2,1)} %get-tuple-element.192, s32[]{:T(128)} %get-tuple-element.179), kind=kOutput, calls=%fused_computation.1.clone.1 | convolution fusion | flops 135265280 | bytes 2494976 | tf_op jit(solution)/shard_map/while/body/eval_jaxpr/pkgd,skd->kgps/dot_general | solution.py:98
  191.7 3.2 %fusion.98 = f32[1,4,256,128]{3,2,1,0:T(8,128)} fusion(f32[512,256,4]{1,0,2:T(8,128)} %get-tuple-element.168, f32[4,256]{1,0:T(4,128)S(1)} %bitcast.93, f32[1,4,256,128]{3,2,1,0:T(8,128)} %get-tuple-element.182, f32[4,256]{1,0:T(4,128)S(1)} %get-tuple-element.169, pred[]{:T(512)S(6)} %compare.4, bf16[4,512,1,128]{3,1,2,0:T(8,128)(2,1)} %get-tuple-element.194, ...), kind=kOutput, calls=%fused_computation.6.clone.1 | convolution fusion | flops 136183808 | bytes 3285505 | tf_op jit(solution)/shard_map/while/body/eval_jaxpr/kgps,skd->kgpd/dot_general | solution.py:105
  195.3 2.1 copy.15
  197.4 1.1 divide_convert_fusion
  198.4 1.5 convolution_convert_fusion
  199.9 7.0 %reduce-scatter.8.cloned.1.call-done = bf16[256,768]{1,0:T(8,128)(2,1)} async-done(((bf16[256,1536]{1,0:T(8,128)(2,1)}), bf16[256,768]{1,0:T(8,128)(2,1)}) %reduce-scatter.8.cloned.1.call-update) | async-done | bytes 393232 | tf_op jit(solution)/shard_map/reduce_scatter | solution.py:137
  206.9 2.1 add_convert_fusion
  (76 shorter events, 1.3 us)
Async XLA Ops:
  6.5 191.9 %copy-start = (bf16[512,1536]{1,0:T(8,128)(2,1)S(1)}, bf16[512,1536]{1,0:T(8,128)(2,1)}, u32[]{:S(2)}) copy-start(bf16[512,1536]{1,0:T(8,128)(2,1)} %param.17) | copy-start | bytes 4718596
  6.5 22.4 %copy-start.2 = (bf16[256,768]{1,0:T(8,128)(2,1)S(1)}, bf16[256,768]{1,0:T(8,128)(2,1)}, u32[]{:S(2)}) copy-start(bf16[256,768]{1,0:T(8,128)(2,1)} %param.10) | copy-start | bytes 1179652
  6.5 41.2 %reduce-scatter.4.cloned.1.call-start = ((), (), s32[]{:S(2)}) async-start(), calls=%async_computation.3 | async-start | bytes 4718592 | tf_op jit(solution)/shard_map/reduce_scatter | solution.py:41
  7.8 17.4 %collective-permute-start = (bf16[192,768]{1,0:T(8,128)(2,1)S(1)}, bf16[192,768]{1,0:T(8,128)(2,1)S(1)}, u32[]{:S(2)}, u32[]{:S(2)}) collective-permute-start(bf16[192,768]{1,0:T(8,128)(2,1)S(1)} %get-tuple-element.115), channel_id=1, source_target_pairs={{0,2},{2,4},{4,6},{6,8},{8,10},{10,12},{12,14},{1,3},{3,5},{5,7},{... | collective-permute-start | bytes 884744 | tf_op jit(solution)/shard_map/ppermute | solution.py:18
  12.7 12.6 %collective-permute-start.1 = (bf16[192,768]{1,0:T(8,128)(2,1)S(1)}, bf16[192,768]{1,0:T(8,128)(2,1)S(1)}, u32[]{:S(2)}, u32[]{:S(2)}) collective-permute-start(bf16[192,768]{1,0:T(8,128)(2,1)S(1)} %get-tuple-element.116), channel_id=1, source_target_pairs={{2,0},{4,2},{6,4},{8,6},{10,8},{12,10},{14,12},{3,1},{5,3},{7,5},{... | collective-permute-start | bytes 884744 | tf_op jit(solution)/shard_map/ppermute | solution.py:19
  34.6 32.4 %reduce-scatter.6.cloned.1.call-start = ((), (), s32[]{:S(2)}) async-start(), calls=%async_computation.4 | async-start | bytes 2359296 | tf_op jit(solution)/shard_map/reduce_scatter | solution.py:41
  56.6 14.2 %copy-start.14 = (f32[768]{0:T(1024)S(1)}, f32[768]{0:T(1024)}, u32[]{:S(2)}) copy-start(f32[768]{0:T(1024)} %param.14) | copy-start | bytes 9220
  56.6 150.3 %reduce-scatter.8.cloned.1.call-start = ((), (), s32[]{:S(2)}) async-start(), calls=%async_computation.5 | async-start | bytes 1179648 | tf_op jit(solution)/shard_map/reduce_scatter | solution.py:137
  70.8 4.6 %copy-start.15 = (bf16[1536,2,128]{2,1,0:T(2,128)(2,1)S(1)}, bf16[1536,2,128]{2,1,0:T(2,128)(2,1)}, u32[]{:S(2)}) copy-start(bf16[1536,2,128]{2,1,0:T(2,128)(2,1)} %param.16) | copy-start | bytes 2359300
  74.5 0.9 copy-start.3
  75.8 7.1 %collective-permute-start.2 = (bf16[256,128]{1,0:T(8,128)(2,1)S(1)}, bf16[256,128]{1,0:T(8,128)(2,1)S(1)}, u32[]{:S(2)}, u32[]{:S(2)}) collective-permute-start(bf16[256,128]{1,0:T(8,128)(2,1)S(1)} %slice.155), channel_id=1, source_target_pairs={{0,2},{2,4},{4,6},{6,8},{8,10},{10,12},{12,14},{14,0},{1,3},{3,5},... | collective-permute-start | bytes 196616 | tf_op jit(solution)/shard_map/ppermute | solution.py:123
  82.9 0.6 copy-start.4
  83.5 7.0 %collective-permute-start.3 = (bf16[256,128]{1,0:T(8,128)(2,1)S(1)}, bf16[256,128]{1,0:T(8,128)(2,1)S(1)}, u32[]{:S(2)}, u32[]{:S(2)}) collective-permute-start(bf16[256,128]{1,0:T(8,128)(2,1)S(1)} %collective-permute-done.2), channel_id=1, source_target_pairs={{0,2},{2,4},{4,6},{6,8},{8,10},{10,12},{12,14},{14,0},{1,3},{3,5},... | collective-permute-start | bytes 196616 | tf_op jit(solution)/shard_map/ppermute | solution.py:123
  90.5 0.6 copy-start.6
  91.1 7.0 %collective-permute-start.4 = (bf16[256,128]{1,0:T(8,128)(2,1)S(1)}, bf16[256,128]{1,0:T(8,128)(2,1)S(1)}, u32[]{:S(2)}, u32[]{:S(2)}) collective-permute-start(bf16[256,128]{1,0:T(8,128)(2,1)S(1)} %collective-permute-done.3), channel_id=1, source_target_pairs={{0,2},{2,4},{4,6},{6,8},{8,10},{10,12},{12,14},{14,0},{1,3},{3,5},... | collective-permute-start | bytes 196616 | tf_op jit(solution)/shard_map/ppermute | solution.py:123
  98.1 0.6 copy-start.8
  98.7 7.0 %collective-permute-start.5 = (bf16[256,128]{1,0:T(8,128)(2,1)S(1)}, bf16[256,128]{1,0:T(8,128)(2,1)S(1)}, u32[]{:S(2)}, u32[]{:S(2)}) collective-permute-start(bf16[256,128]{1,0:T(8,128)(2,1)S(1)} %collective-permute-done.4), channel_id=1, source_target_pairs={{0,2},{2,4},{4,6},{6,8},{8,10},{10,12},{12,14},{14,0},{1,3},{3,5},... | collective-permute-start | bytes 196616 | tf_op jit(solution)/shard_map/ppermute | solution.py:123
  105.6 0.6 copy-start.10
  106.3 7.0 %collective-permute-start.6 = (bf16[256,128]{1,0:T(8,128)(2,1)S(1)}, bf16[256,128]{1,0:T(8,128)(2,1)S(1)}, u32[]{:S(2)}, u32[]{:S(2)}) collective-permute-start(bf16[256,128]{1,0:T(8,128)(2,1)S(1)} %collective-permute-done.5), channel_id=1, source_target_pairs={{0,2},{2,4},{4,6},{6,8},{8,10},{10,12},{12,14},{14,0},{1,3},{3,5},... | collective-permute-start | bytes 196616 | tf_op jit(solution)/shard_map/ppermute | solution.py:123
  113.2 7.6 %copy-start.12 = (bf16[256,128]{1,0:T(8,128)(2,1)}, bf16[256,128]{1,0:T(8,128)(2,1)S(1)}, u32[]{:S(2)}) copy-start(bf16[256,128]{1,0:T(8,128)(2,1)S(1)} %collective-permute-done.6) | copy-start | bytes 196612
  113.2 7.6 %collective-permute-start.7 = (bf16[256,128]{1,0:T(8,128)(2,1)S(1)}, bf16[256,128]{1,0:T(8,128)(2,1)}, u32[]{:S(2)}, u32[]{:S(2)}) collective-permute-start(bf16[256,128]{1,0:T(8,128)(2,1)S(1)} %collective-permute-done.6), channel_id=1, source_target_pairs={{0,2},{2,4},{4,6},{6,8},{8,10},{10,12},{12,14},{14,0},{1,3},{3,5},... | collective-permute-start | bytes 196616 | tf_op jit(solution)/shard_map/ppermute | solution.py:123
  120.8 7.3 %collective-permute-start.8 = (bf16[256,128]{1,0:T(8,128)(2,1)}, bf16[256,128]{1,0:T(8,128)(2,1)}, u32[]{:S(2)}, u32[]{:S(2)}) collective-permute-start(bf16[256,128]{1,0:T(8,128)(2,1)} %collective-permute-done.7), channel_id=1, source_target_pairs={{0,2},{2,4},{4,6},{6,8},{8,10},{10,12},{12,14},{14,0},{1,3},{3,5},... | collective-permute-start | bytes 196616 | tf_op jit(solution)/shard_map/ppermute | solution.py:123
  123.8 12.0 %copy-start.13 = (bf16[256,128]{1,0:T(8,128)(2,1)S(1)}, bf16[256,128]{1,0:T(8,128)(2,1)}, u32[]{:S(2)}) copy-start(bf16[256,128]{1,0:T(8,128)(2,1)} %copy-done.12) | copy-start | bytes 196612
  123.8 12.0 %copy-start.11 = (bf16[256,128]{1,0:T(8,128)(2,1)S(1)}, bf16[256,128]{1,0:T(8,128)(2,1)}, u32[]{:S(2)}) copy-start(bf16[256,128]{1,0:T(8,128)(2,1)} %copy-done.10) | copy-start | bytes 196612
  123.9 12.0 %copy-start.9 = (bf16[256,128]{1,0:T(8,128)(2,1)S(1)}, bf16[256,128]{1,0:T(8,128)(2,1)}, u32[]{:S(2)}) copy-start(bf16[256,128]{1,0:T(8,128)(2,1)} %copy-done.8) | copy-start | bytes 196612
  123.9 12.0 %copy-start.7 = (bf16[256,128]{1,0:T(8,128)(2,1)S(1)}, bf16[256,128]{1,0:T(8,128)(2,1)}, u32[]{:S(2)}) copy-start(bf16[256,128]{1,0:T(8,128)(2,1)} %copy-done.6) | copy-start | bytes 196612
  123.9 12.1 %copy-start.5 = (bf16[256,128]{1,0:T(8,128)(2,1)S(1)}, bf16[256,128]{1,0:T(8,128)(2,1)}, u32[]{:S(2)}) copy-start(bf16[256,128]{1,0:T(8,128)(2,1)} %copy-done.4) | copy-start | bytes 196612
  172.8 3.1 %copy-start.1 = (f32[512,256,4]{1,0,2:T(8,128)S(1)}, f32[512,256,4]{1,0,2:T(8,128)}, u32[]{:S(2)}) copy-start(f32[512,256,4]{1,0,2:T(8,128)} %get-tuple-element.168) | copy-start | bytes 6291460 | tf_op jit(solution)/shard_map/while
  179.0 3.2 %copy-start.1 = (f32[512,256,4]{1,0,2:T(8,128)S(1)}, f32[512,256,4]{1,0,2:T(8,128)}, u32[]{:S(2)}) copy-start(f32[512,256,4]{1,0,2:T(8,128)} %get-tuple-element.168) | copy-start | bytes 6291460 | tf_op jit(solution)/shard_map/while
  185.3 3.2 %copy-start.1 = (f32[512,256,4]{1,0,2:T(8,128)S(1)}, f32[512,256,4]{1,0,2:T(8,128)}, u32[]{:S(2)}) copy-start(f32[512,256,4]{1,0,2:T(8,128)} %get-tuple-element.168) | copy-start | bytes 6291460 | tf_op jit(solution)/shard_map/while
  191.7 3.2 %copy-start.1 = (f32[512,256,4]{1,0,2:T(8,128)S(1)}, f32[512,256,4]{1,0,2:T(8,128)}, u32[]{:S(2)}) copy-start(f32[512,256,4]{1,0,2:T(8,128)} %get-tuple-element.168) | copy-start | bytes 6291460 | tf_op jit(solution)/shard_map/while
Sparse Core Ops, SparseCore 0:
  34.7 13.0 reduce-scatter.3
  56.7 10.2 reduce-scatter.5
  200.1 6.8 reduce-scatter.7
